TPU v7x, 128 devices: a whole 4x4x4 slice. The times are simulated.
128 devices in a mesh: pts: 16 (over z, y), freq: 8 (over x, core).
Axes of the slice: x: 4, y: 4, z: 4, core: 2. Of those that a mesh axis runs over, the one named last changes fastest.
Arguments:
- spectra: bfloat16 [128, 5, 4096, 128], P('freq', None, 'pts'), parts along dimension 0, may hold values from -200 to 200, as said below
- weights: float32 [4096], P('pts'), as said below
Outputs:
- mode_shapes: bfloat16 [128, 5, 4096, 128], P('freq', None, 'pts'), parts along dimension 0
There are 8 independent parts, one for each index of `freq`. A program takes and returns all parts, laid end to end along the dimension named above; an argument that names none is the same for every part. Nothing has to cross between parts.
Inputs may be any that keep to these rules, and one draw needn't show every extreme that they name: `spectra`: each row (frequency, variable, point) and each block's column pair has its own scale; the complex columns are independent. `weights`: Positive; their sum is of order one.
All inputs are finite; a program needn't handle non-finite values.
Results may differ from a plain program's by a relative error of at most 0.0054.
Values sent between devices are 32-bit elements; how exact they have to be, the bound alone decides.
No kernel may reach another device: no remote copies, remote signals or barrier semaphores. Data moves between devices by JAX's collectives and lax.ppermute only.
A program may use at most 64 MiB of HBM per device.

v0:
```python
import jax
import jax.numpy as jnp
from jax import lax
from jax.sharding import PartitionSpec as P

NS_STEPS = 10


def split_parts(products):
    half_cols = products.shape[-1] // 2
    top_left = products[:, :half_cols, :half_cols]
    top_right = products[:, :half_cols, half_cols:]
    bottom_left = products[:, half_cols:, :half_cols]
    bottom_right = products[:, half_cols:, half_cols:]
    return (top_left + bottom_right, top_right - bottom_left)


def build_cross(real_part, imag_part):
    upper_row = jnp.concatenate([real_part, imag_part], 2)
    lower_row = jnp.concatenate([-imag_part, real_part], 2)
    return jnp.concatenate([upper_row, lower_row], 1)


def upper_of(cross_gram):
    order = cross_gram.shape[-1]
    places = jnp.arange(order)

    def eliminate(column, carry):
        working, factor = carry
        picker = (places == column).astype(jnp.float32)
        below = (places >= column).astype(jnp.float32)
        current = jnp.sum(working * picker[None, None, :], axis=2) * below[None, :]
        pivot = jnp.sqrt(jnp.sum(current * picker[None, :], axis=1))
        scaled = current / pivot[:, None]
        factor = factor + scaled[:, None, :] * picker[None, :, None]
        working = working - scaled[:, :, None] * scaled[:, None, :]
        return (working, factor)

    start = (cross_gram, jnp.zeros_like(cross_gram))
    working, factor = lax.fori_loop(0, order, eliminate, start)
    return factor


def solve_upper(upper_factor, right_side):
    order = upper_factor.shape[-1]
    places = jnp.arange(order)

    def back_step(count, solved):
        row = order - 1 - count
        picker = (places == row).astype(jnp.float32)
        factor_row = jnp.sum(upper_factor * picker[None, :, None], axis=1)
        side_row = jnp.sum(right_side * picker[None, :, None], axis=1)
        pivot = jnp.sum(factor_row * picker[None, :], axis=1)
        known = jnp.einsum("fj,fjk->fk", factor_row, solved, precision=lax.Precision.HIGHEST)
        value = (side_row - known) / pivot[:, None]
        return solved + picker[None, :, None] * value[:, None, :]

    return lax.fori_loop(0, order, back_step, jnp.zeros_like(right_side))


def gram_of(upper_factor):
    return jnp.einsum("fki,fkj->fij", upper_factor, upper_factor, precision=lax.Precision.HIGHEST)


def local(spectra, weights):
    freq_count, var_count, point_count, col_count = spectra.shape
    root_weights = jnp.sqrt(weights)
    weighted = (root_weights[None, None, :, None] * spectra.astype(jnp.float32)).astype(
        jnp.bfloat16
    )
    flat_rows = weighted.reshape(freq_count, var_count * point_count, col_count)
    products = jnp.einsum("frc,frd->fcd", flat_rows, flat_rows, preferred_element_type=jnp.float32)
    real_part, imag_part = split_parts(products)
    cross_gram = build_cross(real_part, imag_part)
    summed = lax.psum(cross_gram, "pts")
    upper_factor = upper_of(summed)
    frob_norm = jnp.sqrt(jnp.sum(upper_factor * upper_factor, axis=(1, 2)))
    polar = upper_factor / frob_norm[:, None, None]
    for sweep in range(NS_STEPS):
        inner_gram = gram_of(polar)
        polar = 1.5 * polar - 0.5 * jnp.einsum(
            "fij,fjk->fik", polar, inner_gram, precision=lax.Precision.HIGHEST
        )
    mapping = solve_upper(upper_factor, polar).astype(jnp.bfloat16)
    shapes = jnp.einsum("fvpc,fcd->fvpd", spectra, mapping, preferred_element_type=jnp.float32)
    return shapes.astype(jnp.bfloat16)


def solution(mesh):
    in_specs = (P("freq", None, "pts", None), P("pts"))
    out_specs = P("freq", None, "pts", None)
    return jax.shard_map(local, mesh=mesh, in_specs=in_specs, out_specs=out_specs, check_vma=False)
```

profile of v0, /device:TPU:0, one launch (start us, length us, event | category | flops | bytes accessed | tf_op | source)
XLA Modules:
  0.0 935.5 jit_solution(8490604428545319796)
XLA Ops:
  7.2 4.0 multiply_convert_fusion
  14.6 90.1 %all-reduce.2.cloned.1.call-done = f32[16,128,128]{2,1,0:T(8,128)} async-done(((f32[16,128,128]{2,1,0:T(8,128)}), f32[16,128,128]{2,1,0:T(8,128)}) %all-reduce.2.cloned.1.call-update) | async-done | bytes 1048592 | tf_op jit(solution)/shard_map/psum | solution.py:75
  104.7 568.0 %while.32 = (s32[]{:T(128)}, f32[16,128,128]{2,1,0:T(8,128)}, f32[16,128,128]{2,1,0:T(8,128)S(1)}, s32[]{:T(128)}, s32[]{:T(128)}) while((s32[]{:T(128)}, f32[16,128,128]{2,1,0:T(8,128)}, f32[16,128,128]{2,1,0:T(8,128)S(1)}, s32[]{:T(128)}, s32[]{:T(128)}) %tuple.73), condition=%wide.region_4.0_spmd.clone.clone, body=%wide.region_1.0_spmd.clone.clone.sunk | while | flops 1843699 | bytes 5287763 | solution.py:40
  106.5 2.7 select_add_fusion.2
  110.9 2.7 select_add_fusion.2
  115.3 2.7 select_add_fusion.2
  124.2 2.7 select_add_fusion.2
  133.1 2.7 select_add_fusion.2
  137.5 2.7 select_add_fusion.2
  141.9 2.7 select_add_fusion.2
  146.4 2.7 select_add_fusion.2
  150.8 2.7 select_add_fusion.2
  155.2 2.7 select_add_fusion.2
  159.7 2.7 select_add_fusion.2
  164.1 2.7 select_add_fusion.2
  168.5 2.7 select_add_fusion.2
  173.0 2.7 select_add_fusion.2
  177.4 2.7 select_add_fusion.2
  181.8 2.7 select_add_fusion.2
  186.3 2.7 select_add_fusion.2
  190.7 2.7 select_add_fusion.2
  195.1 2.7 select_add_fusion.2
  199.6 2.7 select_add_fusion.2
  208.4 2.7 select_add_fusion.2
  217.3 2.7 select_add_fusion.2
  221.7 2.7 select_add_fusion.2
  226.2 2.7 select_add_fusion.2
  230.6 2.7 select_add_fusion.2
  235.0 2.7 select_add_fusion.2
  239.5 2.7 select_add_fusion.2
  243.9 2.7 select_add_fusion.2
  248.3 2.7 select_add_fusion.2
  252.8 2.7 select_add_fusion.2
  257.2 2.7 select_add_fusion.2
  261.7 2.7 select_add_fusion.2
  266.1 2.7 select_add_fusion.2
  270.5 2.7 select_add_fusion.2
  275.0 2.7 select_add_fusion.2
  279.4 2.7 select_add_fusion.2
  283.8 2.7 select_add_fusion.2
  292.7 2.7 select_add_fusion.2
  301.6 2.7 select_add_fusion.2
  306.0 2.7 select_add_fusion.2
  310.4 2.7 select_add_fusion.2
  314.9 2.7 select_add_fusion.2
  319.3 2.7 select_add_fusion.2
  323.7 2.7 select_add_fusion.2
  328.2 2.7 select_add_fusion.2
  332.6 2.7 select_add_fusion.2
  337.0 2.7 select_add_fusion.2
  341.5 2.7 select_add_fusion.2
  345.9 2.7 select_add_fusion.2
  350.3 2.7 select_add_fusion.2
  354.8 2.7 select_add_fusion.2
  359.2 2.7 select_add_fusion.2
  363.6 2.7 select_add_fusion.2
  368.1 2.7 select_add_fusion.2
  376.9 2.7 select_add_fusion.2
  385.8 2.7 select_add_fusion.2
  390.2 2.7 select_add_fusion.2
  394.7 2.7 select_add_fusion.2
  705.7 208.5 %while.31 = (s32[]{:T(128)}, f32[16,128,128]{2,1,0:T(8,128)S(1)}, f32[16,128,128]{2,1,0:T(8,128)S(1)}, f32[16,128,128]{2,1,0:T(8,128)S(1)}, s32[]{:T(128)}, /*index=5*/s32[]{:T(128)}, s32[]{:T(128)}) while((s32[]{:T(128)}, f32[16,128,128]{2,1,0:T(8,128)S(1)}, f32[16,128,128]{2,1,0:T(8,128)S(1)}, f32[16,128,128]{2,1,0:T(8,128)S(1)}, ...), condition=%wide.region_10.0_spmd.clone, body=%wide.region_6.0_spmd.clone.sunk | while | flops 5247220 | bytes 5318896 | solution.py:58
  914.2 6.4 convert_bitcast_fusion
  920.6 7.8 copy.8
  (1508 shorter events, 652.9 us)
Async XLA Ops:
  6.5 98.1 %all-reduce.2.cloned.1.call-start = ((), (), s32[]{:S(2)}) async-start(), calls=%async_computation | async-start | bytes 2097152 | tf_op jit(solution)/shard_map/psum | solution.py:75
Sparse Core Ops, SparseCore 0:
  14.7 89.9 all-reduce.1
where the time goes:
time: 950 us; the launch traced here: 936 us
  other arithmetic  655 us (69%)
  matrix products  160 us (17%)
  waiting for transfers between devices  90.1 us (9%)
  between operations  13.8 us (1%)
  local copies, waits for them, and re-layouts  9.6 us (1%)
    add x128, other arithmetic, eliminate(): factor = factor + scaled[:, None, :] * picker[None, :, None]  340 us
    reduce_sum x128, other arithmetic, eliminate(): current = jnp.sum(working * picker[None, None, :], axis=2) * below[None, :]  200 us
    dot_general x128, matrix products, back_step(): jnp.einsum('fj,fjk->fk', factor_row, solved, precision=lax.Precision.HIGH...  120 us
    psum x1, waiting for transfers between devices, local(): summed = lax.psum(cross_gram, 'pts')  90.1 us
    reduce_sum x128, other arithmetic, back_step(): factor_row = jnp.sum(upper_factor * picker[None, :, None], axis=1)  33.5 us
    add x128, other arithmetic, back_step(): return solved + picker[None, :, None] * value[:, None, :]  25.6 us
    dot_general x10, matrix products, gram_of(): jnp.einsum('fki,fkj->fij', upper_factor, upper_factor, precision=lax.Prec...  19.4 us
  transfers between devices with their start and end apart: 1, of which 1 were waited for; matrix products, arithmetic and copies ran while one was open for 0% of the time, Pallas kernels for 0%

commit v1 on v0

--- a/solution.py
+++ b/solution.py
@@ -72,7 +72,7 @@
     products = jnp.einsum("frc,frd->fcd", flat_rows, flat_rows, preferred_element_type=jnp.float32)
     real_part, imag_part = split_parts(products)
     cross_gram = build_cross(real_part, imag_part)
-    summed = lax.psum(cross_gram, "pts")
+    summed = jnp.sum(lax.all_gather(cross_gram, "pts"), axis=0)
     upper_factor = upper_of(summed)
     frob_norm = jnp.sqrt(jnp.sum(upper_factor * upper_factor, axis=(1, 2)))
     polar = upper_factor / frob_norm[:, None, None]

time: 950 us -> 563 us (0.59)
  other arithmetic: 655 us -> 249 us
  waiting for transfers between devices: 90.1 us -> 114 us
    add x128, other arithmetic: 340 us -> 81.9 us  [eliminate(): factor = factor + scaled[:, None, :] * picker[None, :, None]]
    reduce_sum x128, other arithmetic: 200 us -> 44.1 us  [eliminate(): current = jnp.sum(working * picker[None, None, :], axis=2) * below[None, :]]
    all_gather x0 -> x1, waiting for transfers between devices: none -> 114 us  [local(): summed = jnp.sum(lax.all_gather(cross_gram, 'pts'), axis=0)]
    psum x1 -> x0, waiting for transfers between devices: 90.1 us -> none  [local(): summed = lax.psum(cross_gram, 'pts')]
where the time goes in v1:
time: 563 us; the launch traced here: 557 us
  other arithmetic  249 us (44%)
  matrix products  160 us (28%)
  waiting for transfers between devices  114 us (20%)
  between operations  13.8 us (2%)
  loops' own time  10.9 us (2%)
  local copies, waits for them, and re-layouts  9.6 us (2%)
    dot_general x128, matrix products, back_step(): jnp.einsum('fj,fjk->fk', factor_row, solved, precision=lax.Precision.HIGH...  119 us
    all_gather x1, waiting for transfers between devices, local(): summed = jnp.sum(lax.all_gather(cross_gram, 'pts'), axis=0)  114 us
    add x128, other arithmetic, eliminate(): factor = factor + scaled[:, None, :] * picker[None, :, None]  81.9 us
    reduce_sum x128, other arithmetic, eliminate(): current = jnp.sum(working * picker[None, None, :], axis=2) * below[None, :]  44.1 us
    reduce_sum x128, other arithmetic, back_step(): factor_row = jnp.sum(upper_factor * picker[None, :, None], axis=1)  33.5 us
    add x128, other arithmetic, back_step(): return solved + picker[None, :, None] * value[:, None, :]  25.8 us
    dot_general x10, matrix products, gram_of(): jnp.einsum('fki,fkj->fij', upper_factor, upper_factor, precision=lax.Prec...  19.4 us
    reduce_sum x128, other arithmetic, eliminate(): pivot = jnp.sqrt(jnp.sum(current * picker[None, :], axis=1))  14.6 us
  transfers between devices with their start and end apart: 1, of which 1 were waited for; matrix products, arithmetic and copies ran while one was open for 0% of the time, Pallas kernels for 0%

profile of v1, /device:TPU:0, one launch (start us, length us, event | category | flops | bytes accessed | tf_op | source)
XLA Modules:
  0.0 556.8 jit_solution(7274754145352786880)
XLA Ops:
  7.2 4.0 multiply_convert_fusion
  11.3 1.6 fusion.23
  13.3 1.3 maximum_maximum_fusion
  14.6 114.0 %all-gather.3.cloned.1.call-done = f32[256,128,128]{2,1,0:T(8,128)} async-done(((f32[16,128,128]{2,1,0:T(8,128)}), f32[256,128,128]{2,1,0:T(8,128)}) %all-gather.3.cloned.1.call-update) | async-done | bytes 16777232 | tf_op jit(solution)/shard_map/all_gather | solution.py:75
  128.6 7.4 %reduce_sum.83 = f32[16,128,128]{2,1,0:T(8,128)S(1)} reduce(f32[16,16,128,128]{3,2,1,0:T(8,128)} %bitcast.62, f32[]{:T(128)} %constant.44.clone.1), dimensions={0}, to_apply=%region_0.0 | reduce | flops 3932160 | bytes 17825796 | tf_op jit(solution)/shard_map/reduce_sum | solution.py:75
  136.0 157.7 %while.32 = (s32[]{:T(128)}, f32[16,128,128]{2,1,0:T(8,128)S(1)}, f32[16,128,128]{2,1,0:T(8,128)S(1)}, s32[]{:T(128)}, s32[]{:T(128)}) while((s32[]{:T(128)}, f32[16,128,128]{2,1,0:T(8,128)S(1)}, f32[16,128,128]{2,1,0:T(8,128)S(1)}, s32[]{:T(128)}, s32[]{:T(128)}) %tuple.73), condition=%wide.region_4.0_spmd.clone.clone, body=%wide.region_1.0_spmd.clone.clone.sunk | while | flops 1843699 | bytes 5287755 | solution.py:40
  294.0 1.9 fusion.21
  295.9 1.4 fusion.18
  297.3 1.9 fusion.24
  299.2 1.3 fusion.17
  300.5 1.9 fusion.25
  302.4 1.3 fusion.16
  303.7 1.9 fusion.26
  305.7 1.5 fusion.15
  307.1 1.9 fusion.27
  309.1 1.3 fusion.14
  310.4 1.9 fusion.28
  312.3 1.3 fusion.13
  313.6 1.9 fusion.29
  315.5 1.3 fusion.12
  316.9 2.1 fusion.30
  319.0 1.3 fusion.11
  320.3 1.9 fusion.31
  322.2 1.3 fusion.10
  323.5 1.9 fusion.32
  325.5 1.3 fusion.9
  326.8 208.8 %while.31 = (s32[]{:T(128)}, f32[16,128,128]{2,1,0:T(8,128)S(1)}, f32[16,128,128]{2,1,0:T(8,128)S(1)}, f32[16,128,128]{2,1,0:T(8,128)S(1)}, s32[]{:T(128)}, /*index=5*/s32[]{:T(128)}, s32[]{:T(128)}) while((s32[]{:T(128)}, f32[16,128,128]{2,1,0:T(8,128)S(1)}, f32[16,128,128]{2,1,0:T(8,128)S(1)}, f32[16,128,128]{2,1,0:T(8,128)S(1)}, ...), condition=%wide.region_10.0_spmd.clone, body=%wide.region_6.0_spmd.clone.sunk | while | flops 5247220 | bytes 5318888 | solution.py:58
  327.1 0.9 fusion.79
  328.7 0.9 fusion.79
  330.3 0.9 fusion.79
  331.9 0.9 fusion.79
  333.6 0.9 fusion.79
  335.2 0.9 fusion.79
  336.8 0.9 fusion.79
  338.5 0.9 fusion.79
  340.1 0.9 fusion.79
  341.7 0.9 fusion.79
  343.4 0.9 fusion.79
  345.0 0.9 fusion.79
  346.6 0.9 fusion.79
  349.9 0.9 fusion.79
  351.5 0.9 fusion.79
  353.1 0.9 fusion.79
  354.8 0.9 fusion.79
  356.4 0.9 fusion.79
  358.0 0.9 fusion.79
  359.7 0.9 fusion.79
  361.3 0.9 fusion.79
  362.9 0.9 fusion.79
  364.6 0.9 fusion.79
  366.2 0.9 fusion.79
  367.8 0.9 fusion.79
  369.5 0.9 fusion.79
  371.1 0.9 fusion.79
  372.7 0.9 fusion.79
  374.4 0.9 fusion.79
  376.0 0.9 fusion.79
  377.6 0.9 fusion.79
  380.9 0.9 fusion.79
  382.5 0.9 fusion.79
  384.1 0.9 fusion.79
  385.8 0.9 fusion.79
  535.5 6.4 %convert_bitcast_fusion = bf16[16,5,256,128]{2,3,1,0:T(8,128)(2,1)} fusion(bf16[16,5,256,128]{3,2,1,0:T(8,128)(2,1)} %param.6, f32[16,128,128]{2,1,0:T(8,128)S(1)} %get-tuple-element.182), kind=kOutput, calls=%fused_computation.21 | convolution fusion | flops 673972224 | bytes 11534336 | tf_op jit(solution)/shard_map/fvpc,fcd->fvpd/dot_general | solution.py:85
  541.9 7.8 %copy.21 = bf16[16,5,256,128]{3,2,1,0:T(8,128)(2,1)} copy(bf16[16,5,256,128]{2,3,1,0:T(8,128)(2,1)} %convert_bitcast_fusion) | data formatting | bytes 10485760 | tf_op jit(solution)/shard_map/convert_element_type | solution.py:86
  (1509 shorter events, 324.2 us)
Async XLA Ops:
  6.5 122.0 %all-gather.3.cloned.1.call-start = ((), (), s32[]{:S(2)}) async-start(), calls=%async_computation | async-start | bytes 17825792 | tf_op jit(solution)/shard_map/all_gather | solution.py:75
Sparse Core Ops, SparseCore 0:
  14.7 113.8 all-gather.2
